TPU v7x, 256 devices: a whole 4x4x8 slice. The times are simulated.
256 devices in a mesh: rep: 16 (over x, z_lo, core), fsdp: 16 (over z_hi, y).
Axes of the slice: x: 4, y: 4, z: 8 (z_hi: 4, z_lo: 2; z = z_hi * 2 + z_lo), core: 2. Of those that a mesh axis runs over, the one named last changes fastest.
Arguments:
- activations: bfloat16 [16, 2, 2816, 2560], P('rep', None, 'fsdp'), may hold values from -6 to 6
- residual: bfloat16 [16, 2, 2816, 5120], P('rep', None, 'fsdp'), may hold values from -6 to 6
- upstream: bfloat16 [16, 2, 2816, 5120], P('rep', None, 'fsdp'), may hold values from -6 to 6
- norm_gain: float32 [5120], replicated, may hold values from 0.5 to 1.5
- params: float32 [16, 128, 40, 5, 128], P('rep', 'fsdp'), may hold values from -6 to 6
- momentum: float32 [16, 128, 40, 5, 128], P('rep', 'fsdp'), may hold values from -6 to 6
- pattern: int32 [40, 5], replicated, may hold values from 0 to 19, as said below
- step_index: int32 [1], replicated, may hold values from 0 to 2999
Outputs:
- params_out: float32 [16, 128, 40, 5, 128], P('rep', 'fsdp')
- momentum_out: float32 [16, 128, 40, 5, 128], P('rep', 'fsdp')
Inputs may be any that keep to these rules, and one draw needn't show every extreme that they name: `pattern`: each output block column c lists 5 different input blocks, the first of them c mod 20.
All inputs are finite; a program needn't handle non-finite values.
Results may differ from a plain program's by a relative error of at most 0.012.
Values may be sent and summed in bfloat16 or wider, within the bound.
A program may use at most 128 MiB of HBM per device.

v0:
```python
from functools import partial
import math

import jax
import jax.numpy as jnp
from jax import lax
from jax.sharding import PartitionSpec as P

learn_rate = 0.1
momentum_beta = 0.9
decay_keep = 0.999
epsilon = 1e-06


def as_sent(array):
    return jax.tree.map(lambda a: a.astype(jnp.bfloat16) if a.dtype == jnp.float32 else a, array)


def shifted(array, axis, by):
    devices = lax.axis_size(axis)
    return lax.ppermute(array, axis, [(i, (i + by) % devices) for i in range(devices)])


def norm_backward(pre_norm, upstream_rows, gain):
    inv_rms = lax.rsqrt(jnp.mean(pre_norm * pre_norm, axis=-1, keepdims=True) + epsilon)
    weighted = gain * upstream_rows
    inner_mean = jnp.mean(pre_norm * weighted, axis=-1, keepdims=True)
    return inv_rms * weighted - pre_norm * inv_rms * inv_rms * inv_rms * inner_mean


def gossip(weights, stride):
    stride = stride % lax.axis_size("rep")
    if stride == 0:
        return weights
    partner = jax.tree.map(
        lambda part, own: part.astype(own.dtype), shifted(as_sent(weights), "rep", stride), weights
    )
    return 0.5 * (weights + partner)


def body(activations, residual, upstream, norm_gain, params, momentum, pattern, step_index):
    block_size = params.shape[4]
    per_col = pattern.shape[1]
    out_blocks = pattern.shape[0]
    scaling = 1.0 / math.sqrt(per_col * block_size)
    tok_rows = activations.shape[2]
    model_width = residual.shape[3]
    in_blocks = activations.shape[3] // block_size
    weights_now = params
    moment = momentum
    for step_num in range(activations.shape[1]):
        blocks = activations[0, step_num].reshape(tok_rows, in_blocks, block_size)
        picked = jnp.take(blocks, pattern, axis=1)
        low_weights = weights_now[0].astype(jnp.bfloat16)
        gathered = lax.all_gather(low_weights, "fsdp", axis=0, tiled=True)
        summed = jnp.einsum("tcki,icko->tco", picked, gathered, preferred_element_type=jnp.float32)
        pre_norm = residual[0, step_num].astype(jnp.float32) + scaling * summed.reshape(
            tok_rows, model_width
        )
        grad_pre = norm_backward(pre_norm, upstream[0, step_num].astype(jnp.float32), norm_gain)
        grad_low = grad_pre.astype(jnp.bfloat16).reshape(tok_rows, out_blocks, block_size)
        partial_sum = jnp.einsum(
            "tcki,tco->icko", picked, grad_low, preferred_element_type=jnp.float32
        )
        gradient = lax.psum_scatter(
            partial_sum.astype(jnp.bfloat16), "fsdp", scatter_dimension=0, tiled=True
        ).astype(jnp.float32)
        moment = momentum_beta * moment + (scaling * gradient)[None]
        weights_now = decay_keep * weights_now - learn_rate * moment
        branches = [partial(gossip, stride=1), partial(gossip, stride=2), partial(gossip, stride=4)]
        weights_now = lax.switch((step_index[0] + step_num) % 3, branches, weights_now)
    return (weights_now, moment)


def solution(mesh):
    in_specs = (
        P("rep", None, "fsdp", None),
        P("rep", None, "fsdp", None),
        P("rep", None, "fsdp", None),
        P(),
        P("rep", "fsdp", None, None, None),
        P("rep", "fsdp", None, None, None),
        P(),
        P(),
    )
    out_specs = (P("rep", "fsdp", None, None, None), P("rep", "fsdp", None, None, None))
    return jax.shard_map(body, mesh=mesh, in_specs=in_specs, out_specs=out_specs, check_vma=False)
```

profile of v0, /device:TPU:8, one launch (start us, length us, event | category | flops | bytes accessed | tf_op | source)
XLA Modules:
  0.0 560.6 jit_solution(4306211784209971423)
XLA Ops:
  7.2 2.1 copy.156
  9.3 0.0 reduce-scatter.3.cloned.1.call-start
  9.4 2.5 fusion.78
  11.9 0.5 reshape_squeeze.6
  12.4 0.1 copy.66
  12.6 0.1 copy.65
  12.7 0.1 reshape.171
  12.8 0.1 copy.64
  12.9 4.4 convert_bitcast_fusion.1
  17.3 2.5 copy.93
  19.7 0.6 copy-done.2
  20.4 2.4 convert_bitcast_fusion.2
  22.7 2.5 copy.94
  25.3 9.6 %gather_fusion = bf16[200,176,128]{2,1,0:T(8,128)(2,1)} fusion(bf16[176,20,128]{2,0,1:T(8,128)(2,1)S(1)} %copy.66, s32[1024]{0:T(1024)S(1)} %pad_clamp_fusion), kind=kCustom, calls=%fused_computation.clone | custom fusion | bytes 18023200 | tf_op jit(solution)/shard_map/jit(_take)/gather | solution.py:53
  34.9 84.0 %all-gather.5.cloned.1.call-done = bf16[1,128,40,5,128]{4,1,3,2,0:T(8,128)(2,1)} async-done(((bf16[1,8,40,5,128]{4,1,3,2,0:T(8,128)(2,1)}), bf16[1,128,40,5,128]{4,1,3,2,0:T(8,128)(2,1)}) %all-gather.5.cloned.1.call-update) | async-done | bytes 6553616 | tf_op jit(solution)/shard_map/all_gather | solution.py:55
  118.9 10.4 %fusion.12 = f32[40,176,128,1]{2,1,3,0:T(8,128)} fusion(bf16[40,5,176,128]{3,2,1,0:T(8,128)(2,1)} %bitcast.179, pred[40,5]{1,0:T(8,128)(4,1)S(1)} %copy.64, bf16[1,128,40,5,128]{4,1,3,2,0:T(8,128)(2,1)} %all-gather.5.cloned.1.call-done), kind=kOutput, calls=%fused_computation.23 | convolution fusion | flops 1157939200 | bytes 19169480 | tf_op jit(solution)/shard_map/tcki,icko->tco/dot_general | solution.py:56
  129.3 3.8 multiply_reduce_fusion.1
  133.1 15.0 %fusion.25 = bf16[128,40,5,128]{0,3,2,1:T(8,128)(2,1)} fusion(bf16[40,5,176,128]{3,2,1,0:T(8,128)(2,1)S(1)} %bitcast.180, pred[40,5]{1,0:T(8,128)(4,1)S(1)} %copy.64, f32[176,40,128]{2,1,0:T(8,128)} %bitcast.182, f32[176,40,128]{2,1,0:T(8,128)} %bitcast.181, f32[40,176,128,1]{2,1,3,0:T(8,128)} %fusion.12, f32[176]{0:T(256)S(1)} %get-tuple-element.178, ...), kind=kOutput, calls=%fused_computation.32 | convolution fusion | flops 1170227200 | bytes 26400328 | tf_op jit(solution)/shard_map/tcki,tco->icko/dot_general | solution.py:62
  148.1 11.0 %copy.71 = bf16[128,40,5,128]{3,1,2,0:T(8,128)(2,1)} copy(bf16[128,40,5,128]{0,3,2,1:T(8,128)(2,1)} %fusion.25) | data formatting | bytes 13107200 | tf_op jit(solution)/shard_map/convert_element_type | solution.py:66
  159.9 109.4 %reduce-scatter.3.cloned.1.call-done = bf16[8,40,5,128]{3,1,2,0:T(8,128)(2,1)} async-done(((bf16[128,40,5,128]{3,1,2,0:T(8,128)(2,1)}), bf16[8,40,5,128]{3,1,2,0:T(8,128)(2,1)}) %reduce-scatter.3.cloned.1.call-update) | async-done | bytes 409616 | tf_op jit(solution)/shard_map/reduce_scatter | solution.py:65
  269.3 1.1 bitcast_add_fusion.3
  270.4 0.1 broadcast.147
  270.5 14.6 %conditional.4 = (f32[1,8,40,5,128]{4,2,3,1,0:T(8,128)}, f32[1,8,40,5,128]{4,2,3,1,0:T(8,128)S(1)}, f32[1,8,40,5,128]{4,1,3,2,0:T(8,128)S(1)}) conditional(s32[]{:T(128)} %clamp.7, (f32[1,8,40,5,128]{4,2,3,1,0:T(8,128)S(1)}, f32[1,8,40,5,128]{4,2,3,1,0:T(8,128)S(1)}, f32[1,8,40,5,128]{4,2,3,1,0:T(8,128)S(1)}) %tuple.107, ...), branch_computations={%region_3.5_spmd, %region_4.6_spmd, %region_5.7_spmd} | conditional | flops 819200 | bytes 8192064
  270.5 1.0 fusion.74
  271.6 1.9 collective-permute-start.4
  273.5 10.5 %collective-permute-done.4 = bf16[1,8,40,5,128]{4,2,3,1,0:T(8,128)(2,1)S(1)} collective-permute-done((bf16[1,8,40,5,128]{4,2,3,1,0:T(8,128)(2,1)S(1)}, bf16[1,8,40,5,128]{4,2,3,1,0:T(8,128)(2,1)S(1)}, u32[]{:S(2)}, u32[]{:S(2)}) %collective-permute-start.4) | collective-permute-done | bytes 409632 | tf_op jit(solution)/shard_map/cond/branch_1_fun/ppermute | solution.py:21
  283.9 0.1 copy.89
  284.0 1.1 copy.175
  285.1 1.0 fusion.76
  286.2 0.2 copy-done.7
  286.4 1.5 reshape_squeeze.7
  287.9 1.4 copy.76
  289.3 9.6 %gather_fusion.1 = bf16[200,176,128]{2,1,0:T(8,128)(2,1)} fusion(bf16[176,20,128]{2,0,1:T(8,128)(2,1)S(1)} %copy.76, s32[1024]{0:T(1024)S(1)} %pad_clamp_fusion), kind=kCustom, calls=%fused_computation.1.clone | custom fusion | bytes 18023200 | tf_op jit(solution)/shard_map/jit(_take)/gather | solution.py:53
  298.9 4.6 copy.95
  303.5 2.4 copy.96
  306.0 83.1 %all-gather.7.cloned.1.call-done = bf16[1,128,40,5,128]{4,1,3,2,0:T(8,128)(2,1)} async-done(((bf16[1,8,40,5,128]{4,1,3,2,0:T(8,128)(2,1)}), bf16[1,128,40,5,128]{4,1,3,2,0:T(8,128)(2,1)}) %all-gather.7.cloned.1.call-update) | async-done | bytes 6553616 | tf_op jit(solution)/shard_map/all_gather | solution.py:55
  389.1 10.5 %fusion.8 = f32[40,128,176,1]{1,2,3,0:T(8,128)} fusion(bf16[40,5,176,128]{3,2,1,0:T(8,128)(2,1)} %bitcast.177, pred[40,5]{1,0:T(8,128)(4,1)S(1)} %copy.64, bf16[1,128,40,5,128]{4,1,3,2,0:T(8,128)(2,1)} %all-gather.7.cloned.1.call-done), kind=kOutput, calls=%fused_computation.19 | convolution fusion | flops 1157939200 | bytes 19169480 | tf_op jit(solution)/shard_map/tcki,icko->tco/dot_general | solution.py:56
  399.6 3.4 multiply_reduce_fusion
  403.0 13.2 %fusion.22 = bf16[128,40,5,128]{0,3,2,1:T(8,128)(2,1)} fusion(bf16[40,5,176,128]{3,2,1,0:T(8,128)(2,1)} %bitcast.178, pred[40,5]{1,0:T(8,128)(4,1)S(1)} %copy.64, f32[176,40,128]{2,1,0:T(8,128)} %bitcast.184, f32[176,40,128]{2,1,0:T(8,128)S(1)} %bitcast.183, f32[40,128,176,1]{1,2,3,0:T(8,128)} %fusion.8, f32[176]{0:T(256)S(1)} %broadcast_multiply_fusion, ...), kind=kOutput, calls=%fused_computation.31 | convolution fusion | flops 1170227200 | bytes 26400328 | tf_op jit(solution)/shard_map/tcki,tco->icko/dot_general | solution.py:62
  416.2 10.7 %copy.80 = bf16[128,40,5,128]{3,1,2,0:T(8,128)(2,1)} copy(bf16[128,40,5,128]{0,3,2,1:T(8,128)(2,1)} %fusion.22) | data formatting | bytes 13107200 | tf_op jit(solution)/shard_map/convert_element_type | solution.py:66
  427.0 110.0 %reduce-scatter.5.cloned.1.call-done = bf16[8,40,5,128]{3,1,2,0:T(8,128)(2,1)} async-done(((bf16[128,40,5,128]{3,1,2,0:T(8,128)(2,1)}), bf16[8,40,5,128]{3,1,2,0:T(8,128)(2,1)}) %reduce-scatter.5.cloned.1.call-update) | async-done | bytes 409616 | tf_op jit(solution)/shard_map/reduce_scatter | solution.py:65
  537.0 2.0 bitcast_add_fusion.2
  539.0 13.8 %conditional.5 = (f32[1,8,40,5,128]{4,2,3,1,0:T(8,128)S(1)}) conditional(s32[]{:T(128)} %clamp.6, (f32[1,8,40,5,128]{4,1,3,2,0:T(8,128)S(1)}, f32[1,8,40,5,128]{4,2,3,1,0:T(8,128)S(1)}, f32[1,8,40,5,128]{4,2,3,1,0:T(8,128)}) %tuple.52, (f32[1,8,40,5,128]{4,1,3,2,0:T(8,128)S(1)}, f32[1,8,40,5,128]{4,2,3,1,0:T(8,128)S(1)}, ...), branch_computations={%region_9.11_spmd, %region_10.12_spmd, %region_11.13_spmd} | conditional | flops 2048000 | bytes 8192048 | solution.py:71
  539.0 1.4 fusion.5
  540.4 1.5 collective-permute-start.2
  541.9 9.5 %collective-permute-done.2 = bf16[1,8,40,5,128]{4,2,3,1,0:T(8,128)(2,1)S(1)} collective-permute-done((bf16[1,8,40,5,128]{4,2,3,1,0:T(8,128)(2,1)S(1)}, bf16[1,8,40,5,128]{4,2,3,1,0:T(8,128)(2,1)S(1)}, u32[]{:S(2)}, u32[]{:S(2)}) %collective-permute-start.2) | collective-permute-done | bytes 409632 | tf_op jit(solution)/shard_map/cond/branch_2_fun/ppermute | solution.py:21
  551.3 1.4 add_multiply_fusion.2
  552.8 0.9 copy-done.9
  (36 shorter events, 0.3 us)
Async XLA Ops:
  7.2 111.7 %all-gather.5.cloned.1.call-start = ((), (), s32[]{:S(2)}) async-start(), calls=%async_computation.4 | async-start | bytes 6963200 | tf_op jit(solution)/shard_map/all_gather | solution.py:55
  9.3 3.3 copy-start.12
  9.3 260.0 %reduce-scatter.3.cloned.1.call-start = ((), (), s32[]{:S(2)}) async-start(), calls=%async_computation.2 | async-start | bytes 6963200 | tf_op jit(solution)/shard_map/reduce_scatter | solution.py:65
  17.3 3.1 copy-start.2
  118.9 10.4 %copy-start.3 = (bf16[1,2,176,5120]{3,2,1,0:T(8,128)(2,1)S(1)}, bf16[1,2,176,5120]{3,2,1,0:T(8,128)(2,1)}, u32[]{:S(2)}) copy-start(bf16[1,2,176,5120]{3,2,1,0:T(8,128)(2,1)} %param.17) | copy-start | bytes 10813444
  118.9 10.4 %copy-start.11 = (f32[5120]{0:T(1024)S(1)}, f32[5120]{0:T(1024)}, u32[]{:S(2)}) copy-start(f32[5120]{0:T(1024)} %param.19) | copy-start | bytes 61444
  118.9 14.2 %copy-start = (bf16[200,176,128]{2,1,0:T(8,128)(2,1)S(1)}, bf16[200,176,128]{2,1,0:T(8,128)(2,1)}, u32[]{:S(2)}) copy-start(bf16[200,176,128]{2,1,0:T(8,128)(2,1)} %gather_fusion) | copy-start | bytes 27033604
  159.0 110.3 %copy-start.10 = (f32[1,8,40,5,128]{4,2,3,1,0:T(8,128)S(1)}, f32[1,8,40,5,128]{4,2,3,1,0:T(8,128)}, u32[]{:S(2)}) copy-start(f32[1,8,40,5,128]{4,2,3,1,0:T(8,128)} %param.21) | copy-start | bytes 2457604
  159.0 111.5 %copy-start.6 = (f32[1,8,40,5,128]{4,2,3,1,0:T(8,128)S(1)}, f32[1,8,40,5,128]{4,2,3,1,0:T(8,128)}, u32[]{:S(2)}) copy-start(f32[1,8,40,5,128]{4,2,3,1,0:T(8,128)} %param.20) | copy-start | bytes 2457604
  159.1 230.0 %all-gather.7.cloned.1.call-start = ((), (), s32[]{:S(2)}) async-start(), calls=%async_computation.5 | async-start | bytes 6963200 | tf_op jit(solution)/shard_map/all_gather | solution.py:55
  271.6 12.4 %collective-permute-start.4 = (bf16[1,8,40,5,128]{4,2,3,1,0:T(8,128)(2,1)S(1)}, bf16[1,8,40,5,128]{4,2,3,1,0:T(8,128)(2,1)S(1)}, u32[]{:S(2)}, u32[]{:S(2)}) collective-permute-start(bf16[1,8,40,5,128]{4,2,3,1,0:T(8,128)(2,1)S(1)} %get-tuple-element.165), channel_id=1, source_target_pairs={{0,32},{16,48},{32,64},{48,80},{64,96},{80,112},{96,128},{112,144}... | collective-permute-start | bytes 1228808 | tf_op jit(solution)/shard_map/cond/branch_1_fun/ppermute | solution.py:21
  285.1 1.3 copy-start.7
  286.1 250.8 %reduce-scatter.5.cloned.1.call-start = ((), (), s32[]{:S(2)}) async-start(), calls=%async_computation.3 | async-start | bytes 6963200 | tf_op jit(solution)/shard_map/reduce_scatter | solution.py:65
  298.9 4.6 copy-start.1
  389.1 10.5 %copy-start.4 = (bf16[1,2,176,5120]{3,2,1,0:T(8,128)(2,1)S(1)}, bf16[1,2,176,5120]{3,2,1,0:T(8,128)(2,1)}, u32[]{:S(2)}) copy-start(bf16[1,2,176,5120]{3,2,1,0:T(8,128)(2,1)} %param.17) | copy-start | bytes 10813444
  389.1 10.5 %copy-start.5 = (bf16[1,2,176,5120]{3,2,1,0:T(8,128)(2,1)S(1)}, bf16[1,2,176,5120]{3,2,1,0:T(8,128)(2,1)}, u32[]{:S(2)}) copy-start(bf16[1,2,176,5120]{3,2,1,0:T(8,128)(2,1)} %param.18) | copy-start | bytes 10813444
  399.6 3.5 copy-start.8
  540.4 10.9 %collective-permute-start.2 = (bf16[1,8,40,5,128]{4,2,3,1,0:T(8,128)(2,1)S(1)}, bf16[1,8,40,5,128]{4,2,3,1,0:T(8,128)(2,1)S(1)}, u32[]{:S(2)}, u32[]{:S(2)}) collective-permute-start(bf16[1,8,40,5,128]{4,2,3,1,0:T(8,128)(2,1)S(1)} %fusion.5), channel_id=1, source_target_pairs={{0,64},{16,80},{32,96},{48,112},{64,128},{80,144},{96,160},{112,17... | collective-permute-start | bytes 1228808 | tf_op jit(solution)/shard_map/cond/branch_2_fun/ppermute | solution.py:21
  552.8 0.9 copy-start.9
Sparse Core Ops, SparseCore 0:
  10.9 107.8 all-gather.4
  159.2 110.0 reduce-scatter.2
  286.3 102.8 all-gather.6
  427.1 109.8 reduce-scatter.4
where the time goes:
time: 569 us; the launch traced here: 561 us
  waiting for transfers between devices  406 us (71%)
  local copies, waits for them, and re-layouts  64.4 us (11%)
  matrix products  49 us (9%)
  other arithmetic  22 us (4%)
  between operations  15.1 us (3%)
    reduce_scatter x2, waiting for transfers between devices, body(): lax.psum_scatter(partial_sum.astype(jnp.bfloat16), 'fsdp', scatter_dimens...  219 us
    all_gather x2, waiting for transfers between devices, body(): gathered = lax.all_gather(low_weights, 'fsdp', axis=0, tiled=True)  167 us
    dot_general x2, matrix products, body(): jnp.einsum('tcki,tco->icko', picked, grad_low, preferred_element_type=jnp...  28.2 us
    convert_element_type x2, local copies, waits for them, and re-layouts, body(): partial_sum.astype(jnp.bfloat16)  21.7 us
    dot_general x2, matrix products, body(): jnp.einsum('tcki,icko->tco', picked, gathered, preferred_element_type=jnp...  20.8 us
    ppermute x2, waiting for transfers between devices, shifted(): lax.ppermute(array, axis, [(i, (i + by) % devices) for i in range(devices)])  19.9 us
    gather x2, local copies, waits for them, and re-layouts, body(): picked = jnp.take(blocks, pattern, axis=1)  19.2 us
    unnamed x31, local copies, waits for them, and re-layouts  15.9 us
  transfers between devices with their start and end apart: 6, of which 6 were waited for; matrix products, arithmetic and copies ran while one was open for 8% of the time, Pallas kernels for 0%

commit v1 on v0

v1 whole, which is shorter than its diff:
```python
from functools import partial
import math

import jax
import jax.numpy as jnp
from jax import lax
from jax.experimental import pallas as pl
from jax.experimental.pallas import tpu as pltpu
from jax.sharding import PartitionSpec as P

learn_rate = 0.1
momentum_beta = 0.9
decay_keep = 0.999
epsilon = 1e-06

BF = jnp.bfloat16
F32 = jnp.float32
MESH = pl.DeviceIdType.MESH

SIDE = 4
COLS = 2
B_EVERY = 5
AG_LAG = (2, 4, 6, 8)
RS_LAG = (2, 4, 6, 8)


def mod4(v):
    return lax.rem(v + 2 * SIDE, SIDE)


def step_kernel(
    step, scaling, pat, wl, act_hbm, res_hbm, up_hbm, gain, out,
    gat, par, pre, act, act_t, res, up, ssq, spg, relay_in, first_in, last_in, last_relay,
    sems, local_sems,
):
    n_col, per_col = wl.shape[0], wl.shape[1]
    in_blocks, rows = act.shape[0], act.shape[1]
    chunks = n_col // COLS
    width = n_col * 128

    me = lax.axis_index("fsdp")
    zh, y = me // SIDE, lax.rem(me, SIDE)

    def device(z_at, y_at):
        return {"fsdp": z_at * SIDE + y_at}

    def cols(j):
        return pl.ds(j * COLS, COLS)

    def remote(src, dst, kind, j, target):
        return pltpu.make_async_remote_copy(
            src_ref=src, dst_ref=dst, send_sem=sems.at[2 * kind, j], recv_sem=sems.at[2 * kind + 1, j],
            device_id=target, device_id_type=MESH,
        )

    own = pltpu.make_async_copy(wl, gat.at[zh, y], local_sems.at[0])
    own.start()
    loads = [
        pltpu.make_async_copy(res_hbm.at[0, step], res, local_sems.at[1]),
        pltpu.make_async_copy(up_hbm.at[0, step], up, local_sems.at[2]),
    ] + [
        pltpu.make_async_copy(act_hbm.at[0, step, :, pl.ds(b * 128, 128)], act.at[b], local_sems.at[3 + b])
        for b in range(in_blocks)
    ]
    for load in loads:
        load.start()

    barrier = pltpu.get_barrier_semaphore()
    for target in (device(mod4(zh + 1), y), device(mod4(zh - 1), y), device(zh, mod4(y + 1)), device(zh, mod4(y - 1))):
        pl.semaphore_signal(barrier, inc=1, device_id=target, device_id_type=MESH)
    pl.semaphore_wait(barrier, 4)
    own.wait()

    def facts(j):
        y_first = (lax.rem(j, B_EVERY) == B_EVERY - 1).astype(jnp.int32)
        turn = 1 - 2 * lax.rem(j, 2)
        return 1 - y_first, y_first, turn

    def gather_hop1(j, way):
        z_first, y_first, _ = facts(j)
        piece = gat.at[zh, y, cols(j)]
        return remote(piece, piece, 0 if way == 1 else 1, j, device(mod4(zh + way * z_first), mod4(y + way * y_first)))

    def gather_hop1_in(j, turn):
        z_first, y_first, _ = facts(j)
        return gat.at[mod4(zh - turn * z_first), mod4(y - turn * y_first), cols(j)]

    def gather_relay1(j):
        z_first, y_first, turn = facts(j)
        piece = gather_hop1_in(j, turn)
        return remote(piece, piece, 2, j, device(mod4(zh + turn * z_first), mod4(y + turn * y_first)))

    def two_forms(j, z_form, y_form):
        z_first, _, _ = facts(j)
        pl.when(z_first == 1)(z_form)
        pl.when(z_first == 0)(y_form)

    def wait_piece(kind, j):
        piece = gat.at[zh, y, cols(j)]
        remote(piece, piece, kind, j, device(mod4(zh + 1), y)).wait_recv()

    def wait_four(kind, j):
        piece = gat.at[:, y, cols(j)]
        remote(piece, piece, kind, j, device(zh, mod4(y + 1))).wait_recv()

    def wait_by_turn(wait, j, same):
        _, _, turn = facts(j)
        forward = (turn == 1) if same else (turn == -1)
        pl.when(forward)(lambda: wait(0))
        pl.when(jnp.logical_not(forward))(lambda: wait(1))

    def g0(j):
        gather_hop1(j, 1).start()
        gather_hop1(j, -1).start()

    def g1(j):
        wait_by_turn(lambda which: wait_piece(which, j), j, True)
        gather_relay1(j).start()

    def g2(j):
        wait_by_turn(lambda which: wait_piece(which, j), j, False)
        wait_piece(2, j)

        def z_form():
            four = gat.at[:, y, cols(j)]
            remote(four, four, 3, j, device(zh, mod4(y + 1))).start()
            remote(four, four, 4, j, device(zh, mod4(y - 1))).start()

        def y_form():
            four = gat.at[zh, :, cols(j)]
            remote(four, four, 3, j, device(mod4(zh + 1), y)).start()
            remote(four, four, 4, j, device(mod4(zh - 1), y)).start()

        two_forms(j, z_form, y_form)

    def g3(j):
        wait_by_turn(lambda which: wait_four(3 + which, j), j, True)
        _, _, turn = facts(j)

        def z_form():
            four = gat.at[:, mod4(y - turn), cols(j)]
            remote(four, four, 5, j, device(zh, mod4(y + turn))).start()

        def y_form():
            four = gat.at[mod4(zh - turn), :, cols(j)]
            remote(four, four, 5, j, device(mod4(zh + turn), y)).start()

        two_forms(j, z_form, y_form)

    def picked(k):
        return pl.ds(pl.multiple_of(k * 128, 128), 128)

    def forward(c):
        lhs = jnp.concatenate([act[pat[c * per_col + k]] for k in range(per_col)], axis=1)
        rhs = jnp.concatenate(
            [gat[:, :, c, k].astype(F32).reshape(128, 128).astype(BF) for k in range(per_col)], axis=0
        )
        proj = jnp.dot(lhs, rhs, preferred_element_type=F32)
        value = res[:, picked(c)].astype(F32) + scaling * proj
        weighted = gain[pl.ds(c, 1), :] * up[:, picked(c)].astype(F32)
        pre[c] = value
        ssq[...] += value * value
        spg[...] += value * weighted

    def g4(j):
        wait_by_turn(lambda which: wait_four(3 + which, j), j, False)
        wait_four(5, j)
        for q in range(COLS):
            forward(j * COLS + q)

    ssq[...] = jnp.zeros_like(ssq)
    spg[...] = jnp.zeros_like(spg)

    def gather_step(t, carry):
        pl.when(t < chunks)(lambda: g0(t))

        @pl.when(t == 1)
        def _():
            for load in loads:
                load.wait()

        @pl.when(jnp.logical_and(t >= 1, t < 1 + in_blocks // 4))
        def _():
            for q in range(4):
                b = (t - 1) * 4 + q
                act_t[b] = act[b].astype(F32).T.astype(BF)

        for lag, stage in zip(AG_LAG, (g1, g2, g3, g4)):
            j = t - lag
            pl.when(jnp.logical_and(j >= 0, j < chunks))(lambda stage=stage, j=j: stage(j))
        return carry

    lax.fori_loop(0, chunks + AG_LAG[3], gather_step, 0)

    mean_sq = jnp.sum(ssq[...], axis=1, keepdims=True) * (1.0 / width)
    inner = jnp.sum(spg[...], axis=1, keepdims=True) * (1.0 / width)
    inv = lax.rsqrt(mean_sq + epsilon)
    ssq[...] = jnp.broadcast_to(inv, (rows, 128))
    spg[...] = jnp.broadcast_to(inv * inv * inv * inner, (rows, 128))

    def backward(c):
        weighted = gain[pl.ds(c, 1), :] * up[:, picked(c)].astype(F32)
        grad = (ssq[...] * weighted - pre[c] * spg[...]).astype(BF)
        lhs = jnp.concatenate([act_t[pat[c * per_col + k]] for k in range(per_col)], axis=0)
        result = jnp.dot(lhs, grad, preferred_element_type=F32)
        for k in range(per_col):
            par[:, :, c, k] = result[k * 128:(k + 1) * 128].reshape(SIDE, SIDE, 8, 128).astype(BF)

    def s0(j):
        for q in range(COLS):
            backward(j * COLS + q)
        _, _, turn = facts(j)

        def z_form():
            remote(par.at[:, mod4(y + 2), cols(j)], relay_in.at[:, cols(j)], 6, j, device(zh, mod4(y + turn))).start()
            remote(par.at[:, mod4(y - turn), cols(j)], first_in.at[1, :, cols(j)], 7, j, device(zh, mod4(y - turn))).start()

        def y_form():
            remote(par.at[mod4(zh + 2), :, cols(j)], relay_in.at[:, cols(j)], 6, j, device(mod4(zh + turn), y)).start()
            remote(par.at[mod4(zh - turn), :, cols(j)], first_in.at[1, :, cols(j)], 7, j, device(mod4(zh - turn), y)).start()

        two_forms(j, z_form, y_form)

    def s1(j):
        wait_four(6, j)
        _, _, turn = facts(j)

        def z_form():
            at = mod4(y + turn)
            par[:, at, cols(j)] = (par[:, at, cols(j)].astype(F32) + relay_in[:, cols(j)].astype(F32)).astype(BF)
            remote(par.at[:, at, cols(j)], first_in.at[0, :, cols(j)], 8, j, device(zh, at)).start()

        def y_form():
            at = mod4(zh + turn)
            par[at, :, cols(j)] = (par[at, :, cols(j)].astype(F32) + relay_in[:, cols(j)].astype(F32)).astype(BF)
            remote(par.at[at, :, cols(j)], first_in.at[0, :, cols(j)], 8, j, device(at, y)).start()

        two_forms(j, z_form, y_form)

    def s2(j):
        wait_four(7, j)
        wait_four(8, j)
        z_first, y_first, turn = facts(j)
        arrived = first_in[0, :, cols(j)].astype(F32) + first_in[1, :, cols(j)].astype(F32)

        def z_form():
            par[:, y, cols(j)] = (par[:, y, cols(j)].astype(F32) + arrived).astype(BF)

        def y_form():
            par[zh, :, cols(j)] = (par[zh, :, cols(j)].astype(F32) + arrived).astype(BF)

        two_forms(j, z_form, y_form)

        def place(by):
            return mod4(zh + by * z_first), mod4(y + by * y_first)

        far, back = place(2), place(-turn)
        remote(par.at[far[0], far[1], cols(j)], last_relay.at[cols(j)], 9, j, device(*place(turn))).start()
        remote(par.at[back[0], back[1], cols(j)], last_in.at[1, cols(j)], 10, j, device(*back)).start()

    def s3(j):
        wait_piece(9, j)
        z_first, y_first, turn = facts(j)
        at = mod4(zh + turn * z_first), mod4(y + turn * y_first)
        par[at[0], at[1], cols(j)] = (
            par[at[0], at[1], cols(j)].astype(F32) + last_relay[cols(j)].astype(F32)
        ).astype(BF)
        remote(par.at[at[0], at[1], cols(j)], last_in.at[0, cols(j)], 11, j, device(*at)).start()

    def s4(j):
        wait_piece(10, j)
        wait_piece(11, j)
        out[cols(j)] = (
            par[zh, y, cols(j)].astype(F32) + last_in[0, cols(j)].astype(F32) + last_in[1, cols(j)].astype(F32)
        )

    def scatter_step(t, carry):
        pl.when(t < chunks)(lambda: s0(t))
        for lag, stage in zip(RS_LAG, (s1, s2, s3, s4)):
            j = t - lag
            pl.when(jnp.logical_and(j >= 0, j < chunks))(lambda stage=stage, j=j: stage(j))
        return carry

    lax.fori_loop(0, chunks + RS_LAG[3], scatter_step, 0)

    def finish(j, carry):
        piece, four = gat.at[zh, y, cols(j)], gat.at[:, y, cols(j)]
        for kind, ref in ((0, piece), (1, piece), (2, piece), (3, four), (4, four), (5, four),
                          (6, four), (7, four), (8, four), (9, piece), (10, piece), (11, piece)):
            remote(ref, ref, kind, j, device(mod4(zh + 1), y)).wait_send()
        return carry

    lax.fori_loop(0, chunks, finish, 0)


def gradient_of(step, low_weights, activations, residual, upstream, norm_gain, pattern):
    n_col, per_col = pattern.shape
    rows, features = activations.shape[2], activations.shape[3]
    width = residual.shape[3]
    chunks = n_col // COLS
    scaling = 1.0 / math.sqrt(per_col * 128)
    piece = (n_col, per_col, 8, 128)
    vmem, hbm, smem = pltpu.VMEM, pl.ANY, pltpu.SMEM
    return pl.pallas_call(
        partial(step_kernel, step, scaling),
        out_shape=jax.ShapeDtypeStruct(piece, F32),
        in_specs=[
            pl.BlockSpec(memory_space=smem),
            pl.BlockSpec(memory_space=hbm),
            pl.BlockSpec(memory_space=hbm),
            pl.BlockSpec(memory_space=hbm),
            pl.BlockSpec(memory_space=hbm),
            pl.BlockSpec(memory_space=vmem),
        ],
        out_specs=pl.BlockSpec(memory_space=vmem),
        scratch_shapes=[
            vmem((SIDE, SIDE) + piece, BF),
            vmem((SIDE, SIDE) + piece, BF),
            vmem((n_col, rows, 128), F32),
            vmem((features // 128, rows, 128), BF),
            vmem((features // 128, 128, rows), BF),
            vmem((rows, width), BF),
            vmem((rows, width), BF),
            vmem((rows, 128), F32),
            vmem((rows, 128), F32),
            vmem((SIDE,) + piece, BF),
            vmem((2, SIDE) + piece, BF),
            vmem((2,) + piece, BF),
            vmem(piece, BF),
            pltpu.SemaphoreType.DMA((24, chunks)),
            pltpu.SemaphoreType.DMA((3 + features // 128,)),
        ],
        compiler_params=pltpu.CompilerParams(
            collective_id=step, has_side_effects=True, vmem_limit_bytes=60 * 1024 * 1024
        ),
        name="step",
    )(pattern.reshape(-1), low_weights, activations, residual, upstream, norm_gain.reshape(n_col, 128))


def gossip(weights, stride):
    devices = lax.axis_size("rep")
    stride = stride % devices
    if stride == 0:
        return weights
    partner = lax.ppermute(weights.astype(BF), "rep", [(i, (i + stride) % devices) for i in range(devices)])
    return 0.5 * (weights + partner.astype(F32))


def body(activations, residual, upstream, norm_gain, params, momentum, pattern, step_index):
    per_col = pattern.shape[1]
    scaling = 1.0 / math.sqrt(per_col * 128)
    weights_now = params
    moment = momentum
    for step_num in range(activations.shape[1]):
        low_weights = weights_now[0].astype(BF).transpose(1, 2, 0, 3)
        total = gradient_of(step_num, low_weights, activations, residual, upstream, norm_gain, pattern)
        gradient = total.transpose(2, 0, 1, 3)
        moment = momentum_beta * moment + (scaling * gradient)[None]
        weights_now = decay_keep * weights_now - learn_rate * moment
        branches = [partial(gossip, stride=1), partial(gossip, stride=2), partial(gossip, stride=4)]
        weights_now = lax.switch((step_index[0] + step_num) % 3, branches, weights_now)
    return (weights_now, moment)


def solution(mesh):
    in_specs = (
        P("rep", None, "fsdp", None),
        P("rep", None, "fsdp", None),
        P("rep", None, "fsdp", None),
        P(),
        P("rep", "fsdp", None, None, None),
        P("rep", "fsdp", None, None, None),
        P(),
        P(),
    )
    out_specs = (P("rep", "fsdp", None, None, None), P("rep", "fsdp", None, None, None))
    return jax.shard_map(body, mesh=mesh, in_specs=in_specs, out_specs=out_specs, check_vma=False)
```

time: 569 us -> 307 us (0.54)
  waiting for transfers between devices: 406 us -> 19.5 us
  Pallas kernels: 0 us -> 269 us
  local copies, waits for them, and re-layouts: 64.4 us -> 5.92 us
  matrix products: 49 us -> 0 us
  other arithmetic: 22 us -> 5.53 us
  between operations: 15.1 us -> 1.38 us
    pallas_call x0 -> x2, Pallas kernels: none -> 269 us  [gradient_of(): pl.pallas_call(partial(step_kernel, step, scaling), out_shape=jax.ShapeDt...]
    reduce_scatter x2 -> x0, waiting for transfers between devices: 219 us -> none  [body(): lax.psum_scatter(partial_sum.astype(jnp.bfloat16), 'fsdp', scatter_dimens...]
    all_gather x2 -> x0, waiting for transfers between devices: 167 us -> none  [body(): gathered = lax.all_gather(low_weights, 'fsdp', axis=0, tiled=True)]
    dot_general x4 -> x0, matrix products: 49 us -> none  [the longest x2 28.2 us: body(): jnp.einsum('tcki,tco->icko', picked, grad_low, preferred_element_type=jnp...]
    convert_element_type x2 -> x0, local copies, waits for them, and re-layouts: 21.7 us -> none  [body(): partial_sum.astype(jnp.bfloat16)]
    gather x2 -> x0, local copies, waits for them, and re-layouts: 19.2 us -> none  [body(): picked = jnp.take(blocks, pattern, axis=1)]
    unnamed x31 -> x9, local copies, waits for them, and re-layouts: 15.9 us -> 3.99 us
    reduce_sum x2 -> x0, other arithmetic: 7.21 us -> none  [norm_backward(): jnp.mean(pre_norm * pre_norm, axis=-1, keepdims=True) + epsilon]
  transfers between devices with their start and end apart: 6 -> 2, of which waited for: 6 -> 2; matrix products, arithmetic and copies ran while one was open for 8% -> 0% of each run, Pallas kernels for 0% -> 0%
where the time goes in v1:
time: 307 us; the launch traced here: 301 us
  Pallas kernels  269 us (88%)
  waiting for transfers between devices  19.5 us (6%)
  local copies, waits for them, and re-layouts  5.92 us (2%)
  other arithmetic  5.53 us (2%)
    pallas_call x2, Pallas kernels, gradient_of(): pl.pallas_call(partial(step_kernel, step, scaling), out_shape=jax.ShapeDt...  269 us
    ppermute x2, waiting for transfers between devices, gossip(): lax.ppermute(weights.astype(BF), 'rep', [(i, (i + stride) % devices) for...  19.5 us
  transfers between devices with their start and end apart: 2, of which 2 were waited for; matrix products, arithmetic and copies ran while one was open for 0% of the time, Pallas kernels for 0%

profile of v1, /device:TPU:8, one launch (start us, length us, event | category | flops | bytes accessed | tf_op | source)
XLA Modules:
  0.0 301.3 jit_solution(4171960627023234402)
XLA Ops:
  1.3 0.8 copy.48
  2.1 0.7 reshape.32.pat
  2.8 2.1 copy.129
  4.8 0.0 copy-start.2
  4.8 0.0 copy-start
  4.8 138.5 %step.2 = f32[40,5,8,128]{3,2,1,0:T(8,128)} custom-call(s32[200]{0:T(256)} %reshape.32.pat, bf16[40,5,8,128]{3,2,1,0:T(8,128)(2,1)} %bitcast.20, bf16[1,2,176,2560]{3,2,1,0:T(8,128)(2,1)} %act_hbm.3, bf16[1,2,176,5120]{3,2,1,0:T(8,128)(2,1)} %res_hbm.3, bf16[1,2,176,5120]{3,2,1,0:T(8,128)(2,1)} %up_hbm.3, f32[40,128]{1,0:T(8,128)} %bitcast.21), custom_call_target="tpu_custom_call" | custom-call | tf_op jit(solution)/shard_map/step/pallas_call | solution.py:304
  143.3 0.0 copy-done.2
  143.3 1.4 bitcast_add_fusion.1
  144.7 0.1 broadcast.46
  144.8 0.0 copy-done
  144.8 11.9 %conditional.4 = (f32[1,8,40,5,128]{4,2,3,1,0:T(8,128)}, f32[1,8,40,5,128]{4,2,3,1,0:T(8,128)S(1)}, f32[1,8,40,5,128]{4,1,3,2,0:T(8,128)S(1)}) conditional(s32[]{:T(128)} %clamp.7, (f32[1,8,40,5,128]{4,2,3,1,0:T(8,128)S(1)}, f32[1,8,40,5,128]{4,2,3,1,0:T(8,128)S(1)}, f32[1,8,40,5,128]{4,1,3,2,0:T(8,128)S(1)}) %tuple.96, ...), branch_computations={%region_0.1_spmd, %region_1.2_spmd, %region_2.3_spmd} | conditional | flops 819200 | bytes 8192064
  144.8 1.1 fusion.11
  145.9 0.0 collective-permute-start.3
  146.0 9.5 %collective-permute-done.3 = bf16[1,8,40,5,128]{4,2,3,1,0:T(8,128)(2,1)S(1)} collective-permute-done((bf16[1,8,40,5,128]{4,2,3,1,0:T(8,128)(2,1)S(1)}, bf16[1,8,40,5,128]{4,2,3,1,0:T(8,128)(2,1)S(1)}, u32[]{:S(2)}, u32[]{:S(2)}) %collective-permute-start.3) | collective-permute-done | bytes 409632 | tf_op jit(solution)/shard_map/cond/branch_0_fun/ppermute | solution.py:345
  155.4 0.1 copy.62
  155.5 1.1 copy.146
  156.6 1.0 convert_bitcast_fusion
  157.6 130.3 %step.3 = f32[40,5,8,128]{3,2,1,0:T(8,128)} custom-call(s32[200]{0:T(256)} %reshape.32.pat, bf16[40,5,8,128]{3,2,1,0:T(8,128)(2,1)} %get-tuple-element.175.wl, bf16[1,2,176,2560]{3,2,1,0:T(8,128)(2,1)} %act_hbm.3, bf16[1,2,176,5120]{3,2,1,0:T(8,128)(2,1)} %res_hbm.3, bf16[1,2,176,5120]{3,2,1,0:T(8,128)(2,1)} %up_hbm.3, f32[40,128]{1,0:T(8,128)} %bitcast.22), custom_call_target="tpu_custom_call" | custom-call | tf_op jit(solution)/shard_map/step/pallas_call | solution.py:304
  287.9 1.3 bitcast_add_fusion
  289.2 10.9 %conditional.5 = (f32[1,8,40,5,128]{4,2,3,1,0:T(8,128)S(1)}) conditional(s32[]{:T(128)} %clamp.6, (f32[1,8,40,5,128]{4,1,3,2,0:T(8,128)S(1)}, f32[1,8,40,5,128]{4,2,3,1,0:T(8,128)S(1)}, f32[1,8,40,5,128]{4,1,3,2,0:T(8,128)S(1)}) %tuple.51, (f32[1,8,40,5,128]{4,1,3,2,0:T(8,128)S(1)}, f32[1,8,40,5,128]{4,2,3,1,0:T(8,128)S(1)}, ...), branch_computations={%region_3.4_spmd, %region_4.5_spmd, %region_5.6_spmd} | conditional | flops 2048000 | bytes 8192048 | solution.py:361
  289.2 0.4 fusion.6
  289.6 0.1 collective-permute-start.1
  289.7 10.0 %collective-permute-done.1 = bf16[1,8,40,5,128]{4,2,3,1,0:T(8,128)(2,1)S(1)} collective-permute-done((bf16[1,8,40,5,128]{4,2,3,1,0:T(8,128)(2,1)S(1)}, bf16[1,8,40,5,128]{4,2,3,1,0:T(8,128)(2,1)S(1)}, u32[]{:S(2)}, u32[]{:S(2)}) %collective-permute-start.1) | collective-permute-done | bytes 409632 | tf_op jit(solution)/shard_map/cond/branch_1_fun/ppermute | solution.py:345
  299.7 0.4 add_multiply_fusion.1
  300.1 0.0 copy-start.1
  300.1 1.2 copy.61
  301.3 0.0 copy-done.1
Async XLA Ops:
  4.8 138.5 %copy-start.2 = (f32[1,8,40,5,128]{4,2,3,1,0:T(8,128)S(1)}, f32[1,8,40,5,128]{4,2,3,1,0:T(8,128)}, u32[]{:S(2)}) copy-start(f32[1,8,40,5,128]{4,2,3,1,0:T(8,128)} %param.19) | copy-start | bytes 2457604
  4.8 140.0 %copy-start = (f32[1,8,40,5,128]{4,2,3,1,0:T(8,128)S(1)}, f32[1,8,40,5,128]{4,2,3,1,0:T(8,128)}, u32[]{:S(2)}) copy-start(f32[1,8,40,5,128]{4,2,3,1,0:T(8,128)} %param.18) | copy-start | bytes 2457604
  145.9 9.5 %collective-permute-start.3 = (bf16[1,8,40,5,128]{4,2,3,1,0:T(8,128)(2,1)S(1)}, bf16[1,8,40,5,128]{4,2,3,1,0:T(8,128)(2,1)S(1)}, u32[]{:S(2)}, u32[]{:S(2)}) collective-permute-start(bf16[1,8,40,5,128]{4,2,3,1,0:T(8,128)(2,1)S(1)} %get-tuple-element.169), channel_id=1, source_target_pairs={{0,16},{16,32},{32,48},{48,64},{64,80},{80,96},{96,112},{112,128},... | collective-permute-start | bytes 1228808 | tf_op jit(solution)/shard_map/cond/branch_0_fun/ppermute | solution.py:345
  289.6 10.1 %collective-permute-start.1 = (bf16[1,8,40,5,128]{4,2,3,1,0:T(8,128)(2,1)S(1)}, bf16[1,8,40,5,128]{4,2,3,1,0:T(8,128)(2,1)S(1)}, u32[]{:S(2)}, u32[]{:S(2)}) collective-permute-start(bf16[1,8,40,5,128]{4,2,3,1,0:T(8,128)(2,1)S(1)} %fusion.6), channel_id=1, source_target_pairs={{0,32},{16,48},{32,64},{48,80},{64,96},{80,112},{96,128},{112,144}... | collective-permute-start | bytes 1228808 | tf_op jit(solution)/shard_map/cond/branch_1_fun/ppermute | solution.py:345
  300.1 1.2 copy-start.1

commit v2 on v1

v2 whole, which is shorter than its diff:
```python
from functools import partial
import math

import jax
import jax.numpy as jnp
from jax import lax
from jax.experimental import pallas as pl
from jax.experimental.pallas import tpu as pltpu
from jax.sharding import PartitionSpec as P

learn_rate = 0.1
momentum_beta = 0.9
decay_keep = 0.999
epsilon = 1e-06

BF = jnp.bfloat16
F32 = jnp.float32
MESH = pl.DeviceIdType.MESH

SIDE = 4
COLS = 2
B_EVERY = 5
AG_LAG = (3, 6, 9, 12)
RS_LAG = (3, 6, 9, 12)
HOP_LAG = 2
STEPS = 2


def mod4(v):
    return lax.rem(v + 2 * SIDE, SIDE)


def steps_kernel(
    hops, scaling, pat, w_in, m_in, act_hbm, res_hbm, up_hbm, gain, w_out, m_out,
    gat, par, pre, act, act_t, res, up, ssq, spg, relay_in, first_in, last_in, last_relay, hop_out, hop_in,
    sems, local_sems,
):
    n_col, per_col = w_in.shape[0], w_in.shape[1]
    in_blocks, rows = act.shape[1], act.shape[2]
    chunks = n_col // COLS
    width = n_col * 128
    replicas = lax.axis_size("rep")

    rep = lax.axis_index("rep")
    me = lax.axis_index("fsdp")
    zh, y = me // SIDE, lax.rem(me, SIDE)

    def device(z_at, y_at):
        return {"fsdp": z_at * SIDE + y_at}

    def cols(j):
        return pl.ds(j * COLS, COLS)

    def remote(src, dst, kind, j, target):
        return pltpu.make_async_remote_copy(
            src_ref=src, dst_ref=dst, send_sem=sems.at[2 * kind, j], recv_sem=sems.at[2 * kind + 1, j],
            device_id=target, device_id_type=MESH,
        )

    def loads(s):
        at = s * (2 + in_blocks)
        return [
            pltpu.make_async_copy(res_hbm.at[0, s], res.at[s], local_sems.at[at]),
            pltpu.make_async_copy(up_hbm.at[0, s], up.at[s], local_sems.at[at + 1]),
        ] + [
            pltpu.make_async_copy(act_hbm.at[0, s, :, pl.ds(b * 128, 128)], act.at[s, b], local_sems.at[at + 2 + b])
            for b in range(in_blocks)
        ]

    for load in loads(0):
        load.start()

    barrier = pltpu.get_barrier_semaphore()
    targets = [device(mod4(zh + 1), y), device(mod4(zh - 1), y), device(zh, mod4(y + 1)), device(zh, mod4(y - 1))]
    for hop in hops:
        targets += [{"rep": lax.rem(rep + hop, replicas)}, {"rep": lax.rem(rep + replicas - hop, replicas)}]
    for target in targets:
        pl.semaphore_signal(barrier, inc=1, device_id=target, device_id_type=MESH)
    gat[zh, y] = w_in[...].astype(BF)
    ssq[...] = jnp.zeros_like(ssq)
    spg[...] = jnp.zeros_like(spg)
    pl.semaphore_wait(barrier, len(targets))

    def facts(j):
        y_first = (lax.rem(j, B_EVERY) == B_EVERY - 1).astype(jnp.int32)
        turn = 1 - 2 * lax.rem(j, 2)
        return 1 - y_first, y_first, turn

    def two_forms(j, z_form, y_form):
        z_first, _, _ = facts(j)
        pl.when(z_first == 1)(z_form)
        pl.when(z_first == 0)(y_form)

    def piece_copy(kind, j):
        piece = gat.at[zh, y, cols(j)]
        return remote(piece, piece, kind, j, device(mod4(zh + 1), y))

    def four_copy(kind, j):
        four = gat.at[:, y, cols(j)]
        return remote(four, four, kind, j, device(zh, mod4(y + 1)))

    def wait_by_turn(copy, kind, j, same):
        _, _, turn = facts(j)
        forward = (turn == 1) if same else (turn == -1)
        pl.when(forward)(lambda: copy(kind, j).wait_recv())
        pl.when(jnp.logical_not(forward))(lambda: copy(kind + 1, j).wait_recv())

    def g0(s, j):
        z_first, y_first, _ = facts(j)
        piece = gat.at[zh, y, cols(j)]
        for kind, way in ((0, 1), (1, -1)):
            remote(piece, piece, kind, j, device(mod4(zh + way * z_first), mod4(y + way * y_first))).start()

    def g1(s, j):
        wait_by_turn(piece_copy, 0, j, True)
        z_first, y_first, turn = facts(j)
        piece = gat.at[mod4(zh - turn * z_first), mod4(y - turn * y_first), cols(j)]
        remote(piece, piece, 2, j, device(mod4(zh + turn * z_first), mod4(y + turn * y_first))).start()

    def g2(s, j):
        wait_by_turn(piece_copy, 0, j, False)
        piece_copy(2, j).wait_recv()

        def z_form():
            four = gat.at[:, y, cols(j)]
            remote(four, four, 3, j, device(zh, mod4(y + 1))).start()
            remote(four, four, 4, j, device(zh, mod4(y - 1))).start()

        def y_form():
            four = gat.at[zh, :, cols(j)]
            remote(four, four, 3, j, device(mod4(zh + 1), y)).start()
            remote(four, four, 4, j, device(mod4(zh - 1), y)).start()

        two_forms(j, z_form, y_form)

    def g3(s, j):
        wait_by_turn(four_copy, 3, j, True)
        _, _, turn = facts(j)

        def z_form():
            four = gat.at[:, mod4(y - turn), cols(j)]
            remote(four, four, 5, j, device(zh, mod4(y + turn))).start()

        def y_form():
            four = gat.at[mod4(zh - turn), :, cols(j)]
            remote(four, four, 5, j, device(mod4(zh + turn), y)).start()

        two_forms(j, z_form, y_form)

    def lanes(c):
        return pl.ds(pl.multiple_of(c * 128, 128), 128)

    def forward(s, c):
        lhs = jnp.concatenate([act[s, pat[c * per_col + k]] for k in range(per_col)], axis=1)
        rhs = jnp.concatenate(
            [gat[:, :, c, k].astype(F32).reshape(128, 128).astype(BF) for k in range(per_col)], axis=0
        )
        proj = jnp.dot(lhs, rhs, preferred_element_type=F32)
        value = res[s, :, lanes(c)].astype(F32) + scaling * proj
        weighted = gain[pl.ds(c, 1), :] * up[s, :, lanes(c)].astype(F32)
        pre[c] = value
        ssq[s] += value * value
        spg[s] += value * weighted

    def g4(s, j):
        wait_by_turn(four_copy, 3, j, False)
        four_copy(5, j).wait_recv()
        for q in range(COLS):
            forward(s, j * COLS + q)
        for kind in range(3):
            piece_copy(kind, j).wait_send()
            four_copy(3 + kind, j).wait_send()

    def norm(s):
        inv = lax.rsqrt(jnp.sum(ssq[s], axis=1, keepdims=True) * (1.0 / width) + epsilon)
        inner = jnp.sum(spg[s], axis=1, keepdims=True) * (1.0 / width)
        ssq[s] = jnp.broadcast_to(inv, (rows, 128))
        spg[s] = jnp.broadcast_to(inv * inv * inv * inner, (rows, 128))

    def backward(s, c):
        weighted = gain[pl.ds(c, 1), :] * up[s, :, lanes(c)].astype(F32)
        grad = (ssq[s] * weighted - pre[c] * spg[s]).astype(BF)
        lhs = jnp.concatenate([act_t[s, pat[c * per_col + k]] for k in range(per_col)], axis=0)
        result = jnp.dot(lhs, grad, preferred_element_type=F32)
        for k in range(per_col):
            par[:, :, c, k] = result[k * 128:(k + 1) * 128].reshape(SIDE, SIDE, 8, 128).astype(BF)

    def s0(s, j):
        for q in range(COLS):
            backward(s, j * COLS + q)
        _, _, turn = facts(j)

        def z_form():
            remote(par.at[:, mod4(y + 2), cols(j)], relay_in.at[:, cols(j)], 6, j, device(zh, mod4(y + turn))).start()
            remote(par.at[:, mod4(y - turn), cols(j)], first_in.at[1, :, cols(j)], 7, j, device(zh, mod4(y - turn))).start()

        def y_form():
            remote(par.at[mod4(zh + 2), :, cols(j)], relay_in.at[:, cols(j)], 6, j, device(mod4(zh + turn), y)).start()
            remote(par.at[mod4(zh - turn), :, cols(j)], first_in.at[1, :, cols(j)], 7, j, device(mod4(zh - turn), y)).start()

        two_forms(j, z_form, y_form)

    def s1(s, j):
        four_copy(6, j).wait_recv()
        _, _, turn = facts(j)

        def z_form():
            at = mod4(y + turn)
            par[:, at, cols(j)] = (par[:, at, cols(j)].astype(F32) + relay_in[:, cols(j)].astype(F32)).astype(BF)
            remote(par.at[:, at, cols(j)], first_in.at[0, :, cols(j)], 8, j, device(zh, at)).start()

        def y_form():
            at = mod4(zh + turn)
            par[at, :, cols(j)] = (par[at, :, cols(j)].astype(F32) + relay_in[:, cols(j)].astype(F32)).astype(BF)
            remote(par.at[at, :, cols(j)], first_in.at[0, :, cols(j)], 8, j, device(at, y)).start()

        two_forms(j, z_form, y_form)

    def s2(s, j):
        four_copy(7, j).wait_recv()
        four_copy(8, j).wait_recv()
        z_first, y_first, turn = facts(j)
        arrived = first_in[0, :, cols(j)].astype(F32) + first_in[1, :, cols(j)].astype(F32)

        def z_form():
            par[:, y, cols(j)] = (par[:, y, cols(j)].astype(F32) + arrived).astype(BF)

        def y_form():
            par[zh, :, cols(j)] = (par[zh, :, cols(j)].astype(F32) + arrived).astype(BF)

        two_forms(j, z_form, y_form)

        def place(by):
            return mod4(zh + by * z_first), mod4(y + by * y_first)

        far, back = place(2), place(-turn)
        remote(par.at[far[0], far[1], cols(j)], last_relay.at[cols(j)], 9, j, device(*place(turn))).start()
        remote(par.at[back[0], back[1], cols(j)], last_in.at[1, cols(j)], 10, j, device(*back)).start()

    def s3(s, j):
        piece_copy(9, j).wait_recv()
        z_first, y_first, turn = facts(j)
        at = mod4(zh + turn * z_first), mod4(y + turn * y_first)
        par[at[0], at[1], cols(j)] = (
            par[at[0], at[1], cols(j)].astype(F32) + last_relay[cols(j)].astype(F32)
        ).astype(BF)
        remote(par.at[at[0], at[1], cols(j)], last_in.at[0, cols(j)], 11, j, device(*at)).start()

    def hop_copy(s, j):
        hop = hops[0] + s * (hops[1] - hops[0])
        return remote(hop_out.at[cols(j)], hop_in.at[s, cols(j)], 12 + s, j, {"rep": lax.rem(rep + hop, replicas)})

    def s4(s, j):
        piece_copy(10, j).wait_recv()
        piece_copy(11, j).wait_recv()
        total = (
            par[zh, y, cols(j)].astype(F32) + last_in[0, cols(j)].astype(F32) + last_in[1, cols(j)].astype(F32)
        )
        moment = momentum_beta * m_out[cols(j)] + scaling * total
        weights = decay_keep * w_out[cols(j)] - learn_rate * moment
        m_out[cols(j)] = moment
        w_out[cols(j)] = weights
        hop_out[cols(j)] = weights.astype(BF)
        hop_copy(s, j).start()

    def s5(s, j):
        hop_copy(s, j).wait()
        weights = 0.5 * (w_out[cols(j)] + hop_in[s, cols(j)].astype(F32))
        w_out[cols(j)] = weights

        @pl.when(s == 0)
        def _():
            gat[zh, y, cols(j)] = weights.astype(BF)
            g0(s, j)

        for kind in range(3):
            four_copy(6 + kind, j).wait_send()
            piece_copy(9 + kind, j).wait_send()

    w_out[...] = w_in[...]
    m_out[...] = m_in[...]

    scatter_from = chunks + AG_LAG[3]
    next_gather = scatter_from + RS_LAG[3] + HOP_LAG
    scatter_again = next_gather + scatter_from
    last = scatter_again + chunks + RS_LAG[3] + HOP_LAG

    def run(stage, t, start, period):
        since = t - start
        s = (since >= period).astype(jnp.int32)
        j = since - s * period
        pl.when(jnp.logical_and(j >= 0, j < chunks))(lambda: stage(s, j))

    def iteration(t, carry):
        pl.when(t < chunks)(lambda: g0(0, t))

        @pl.when(t == 1)
        def _():
            for load in loads(0):
                load.wait()
            for load in loads(1):
                load.start()

        @pl.when(t == chunks // 2)
        def _():
            for load in loads(1):
                load.wait()

        for s, start in ((0, 1), (1, chunks // 2)):
            @pl.when(jnp.logical_and(t >= start, t < start + in_blocks // 4))
            def _(s=s, start=start):
                for q in range(4):
                    b = (t - start) * 4 + q
                    act_t[s, b] = act[s, b].astype(F32).T.astype(BF)

        for lag, stage in zip(RS_LAG + (RS_LAG[3] + HOP_LAG,), (s1, s2, s3, s4, s5)):
            run(stage, t, scatter_from + lag, scatter_again - scatter_from)
        run(s0, t, scatter_from, scatter_again - scatter_from)
        for lag, stage in zip(AG_LAG, (g1, g2, g3, g4)):
            run(stage, t, lag, next_gather)

        for s, at in ((0, scatter_from - 1), (1, scatter_again - 1)):
            pl.when(t == at)(lambda s=s: norm(s))
        return carry

    lax.fori_loop(0, last, iteration, 0)


def two_steps(number, hops, weights, moment, activations, residual, upstream, norm_gain, pattern):
    n_col, per_col = pattern.shape
    steps, rows, features = activations.shape[1:]
    width = residual.shape[3]
    chunks = n_col // COLS
    in_blocks = features // 128
    scaling = 1.0 / math.sqrt(per_col * 128)
    piece = (n_col, per_col, 8, 128)
    vmem, hbm, smem = pltpu.VMEM, pl.ANY, pltpu.SMEM
    return pl.pallas_call(
        partial(steps_kernel, hops, scaling),
        out_shape=[jax.ShapeDtypeStruct(piece, F32)] * 2,
        in_specs=[
            pl.BlockSpec(memory_space=smem),
            pl.BlockSpec(memory_space=vmem),
            pl.BlockSpec(memory_space=vmem),
            pl.BlockSpec(memory_space=hbm),
            pl.BlockSpec(memory_space=hbm),
            pl.BlockSpec(memory_space=hbm),
            pl.BlockSpec(memory_space=vmem),
        ],
        out_specs=[pl.BlockSpec(memory_space=vmem)] * 2,
        scratch_shapes=[
            vmem((SIDE, SIDE) + piece, BF),
            vmem((SIDE, SIDE) + piece, BF),
            vmem((n_col, rows, 128), F32),
            vmem((steps, in_blocks, rows, 128), BF),
            vmem((steps, in_blocks, 128, rows), BF),
            vmem((steps, rows, width), BF),
            vmem((steps, rows, width), BF),
            vmem((steps, rows, 128), F32),
            vmem((steps, rows, 128), F32),
            vmem((SIDE,) + piece, BF),
            vmem((2, SIDE) + piece, BF),
            vmem((2,) + piece, BF),
            vmem(piece, BF),
            vmem(piece, BF),
            vmem((steps,) + piece, BF),
            pltpu.SemaphoreType.DMA((2 * (12 + steps), chunks)),
            pltpu.SemaphoreType.DMA((steps * (2 + in_blocks),)),
        ],
        compiler_params=pltpu.CompilerParams(
            collective_id=number, has_side_effects=True, vmem_limit_bytes=60 * 1024 * 1024
        ),
        name="two_steps",
    )(pattern.reshape(-1), weights, moment, activations, residual, upstream, norm_gain.reshape(n_col, 128))


def body(activations, residual, upstream, norm_gain, params, momentum, pattern, step_index):
    weights, moment = (a[0].transpose(1, 2, 0, 3) for a in (params, momentum))
    hops = [1, 2, 4]
    branches = [
        partial(two_steps, first, (hops[first], hops[(first + 1) % 3])) for first in range(3)
    ]
    weights, moment = lax.switch(
        step_index[0] % 3, branches, weights, moment, activations, residual, upstream, norm_gain, pattern
    )
    return tuple(a.transpose(2, 0, 1, 3)[None] for a in (weights, moment))


def solution(mesh):
    in_specs = (
        P("rep", None, "fsdp", None),
        P("rep", None, "fsdp", None),
        P("rep", None, "fsdp", None),
        P(),
        P("rep", "fsdp", None, None, None),
        P("rep", "fsdp", None, None, None),
        P(),
        P(),
    )
    out_specs = (P("rep", "fsdp", None, None, None), P("rep", "fsdp", None, None, None))
    return jax.shard_map(body, mesh=mesh, in_specs=in_specs, out_specs=out_specs, check_vma=False)
```

time: 307 us -> 253 us (0.82); the launches traced: 301 us -> 251 us
  Pallas kernels: 269 us -> 245 us
  waiting for transfers between devices: 19.5 us -> 0 us
  other arithmetic: 5.53 us -> 0 us
    pallas_call x2 -> x1, Pallas kernels: 269 us -> 245 us  [two_steps(): pl.pallas_call(partial(steps_kernel, hops, scaling), out_shape=[jax.Shape...]
    ppermute x2 -> x0, waiting for transfers between devices: 19.5 us -> none  [gossip(): lax.ppermute(weights.astype(BF), 'rep', [(i, (i + stride) % devices) for...]
    unnamed x9 -> x0, local copies, waits for them, and re-layouts: 3.99 us -> none
  transfers between devices with their start and end apart: 2 -> 0, of which waited for: 2 -> 0; matrix products, arithmetic and copies ran while one was open for 0% -> 0% of each run, Pallas kernels for 0% -> 0%
where the time goes in v2:
time: 253 us; the launch traced here: 251 us
  Pallas kernels  245 us (97%)
  local copies, waits for them, and re-layouts  5.24 us (2%)
    pallas_call x1, Pallas kernels, two_steps(): pl.pallas_call(partial(steps_kernel, hops, scaling), out_shape=[jax.Shape...  245 us

profile of v2, /device:TPU:8, one launch (start us, length us, event | category | flops | bytes accessed | tf_op | source)
XLA Modules:
  0.0 251.4 jit_solution(9692086138127022482)
XLA Ops:
  1.3 1.7 copy_bitcast_fusion.2
  3.0 246.3 %conditional.1 = ((f32[40,5,8,128]{3,2,1,0:T(8,128)S(1)}, f32[40,5,8,128]{3,2,1,0:T(8,128)S(1)})) conditional(s32[]{:T(128)} %clamp.3, (s32[40,5]{0,1:T(8,128)}, f32[5120]{0:T(1024)}, f32[40,5,8,128]{3,2,1,0:T(8,128)S(1)}, f32[40,5,8,128]{3,2,1,0:T(8,128)S(1)}, bf16[1,2,176,2560]{3,2,1,0:T(8,128)(2,1)}, ...), branch_computations={%region_0.1_spmd, %region_1.2_spmd, %region_2.3_spmd} | conditional | bytes 3208 | solution.py:383
  3.0 0.8 copy.17
  3.8 0.7 reshape.20.pat
  4.5 244.8 %two_steps.4 = (f32[40,5,8,128]{3,2,1,0:T(8,128)S(1)}, f32[40,5,8,128]{3,2,1,0:T(8,128)S(1)}) custom-call(s32[200]{0:T(256)} %reshape.20.pat, f32[40,5,8,128]{3,2,1,0:T(8,128)S(1)} %get-tuple-element.50.w_in, f32[40,5,8,128]{3,2,1,0:T(8,128)S(1)} %get-tuple-element.51.m_in, bf16[1,2,176,2560]{3,2,1,0:T(8,128)(2,1)} %get-tuple-element.52.act_hbm, ...), custom_call_target="tpu_custom_call" | custom-call | tf_op jit(solution)/shard_map/cond/branch_1_fun/two_steps/pallas_call | solution.py:338
  249.3 1.0 copy.26
  250.4 1.0 copy.25

commit v3 on v2

--- a/solution.py
+++ b/solution.py
@@ -151,7 +151,7 @@
         return pl.ds(pl.multiple_of(c * 128, 128), 128)
 
     def forward(s, c):
-        lhs = jnp.concatenate([act[s, pat[c * per_col + k]] for k in range(per_col)], axis=1)
+        lhs = jnp.concatenate([act[s, pat[k, c]] for k in range(per_col)], axis=1)
         rhs = jnp.concatenate(
             [gat[:, :, c, k].astype(F32).reshape(128, 128).astype(BF) for k in range(per_col)], axis=0
         )
@@ -180,7 +180,7 @@
     def backward(s, c):
         weighted = gain[pl.ds(c, 1), :] * up[s, :, lanes(c)].astype(F32)
         grad = (ssq[s] * weighted - pre[c] * spg[s]).astype(BF)
-        lhs = jnp.concatenate([act_t[s, pat[c * per_col + k]] for k in range(per_col)], axis=0)
+        lhs = jnp.concatenate([act_t[s, pat[k, c]] for k in range(per_col)], axis=0)
         result = jnp.dot(lhs, grad, preferred_element_type=F32)
         for k in range(per_col):
             par[:, :, c, k] = result[k * 128:(k + 1) * 128].reshape(SIDE, SIDE, 8, 128).astype(BF)
@@ -277,9 +277,6 @@
             four_copy(6 + kind, j).wait_send()
             piece_copy(9 + kind, j).wait_send()
 
-    w_out[...] = w_in[...]
-    m_out[...] = m_in[...]
-
     scatter_from = chunks + AG_LAG[3]
     next_gather = scatter_from + RS_LAG[3] + HOP_LAG
     scatter_again = next_gather + scatter_from
@@ -294,7 +291,12 @@
     def iteration(t, carry):
         pl.when(t < chunks)(lambda: g0(0, t))
 
-        @pl.when(t == 1)
+        @pl.when(t == 2)
+        def _():
+            w_out[...] = w_in[...]
+            m_out[...] = m_in[...]
+
+        @pl.when(t == 5)
         def _():
             for load in loads(0):
                 load.wait()
@@ -306,7 +308,7 @@
             for load in loads(1):
                 load.wait()
 
-        for s, start in ((0, 1), (1, chunks // 2)):
+        for s, start in ((0, 5), (1, chunks // 2)):
             @pl.when(jnp.logical_and(t >= start, t < start + in_blocks // 4))
             def _(s=s, start=start):
                 for q in range(4):
@@ -371,7 +373,7 @@
             collective_id=number, has_side_effects=True, vmem_limit_bytes=60 * 1024 * 1024
         ),
         name="two_steps",
-    )(pattern.reshape(-1), weights, moment, activations, residual, upstream, norm_gain.reshape(n_col, 128))
+    )(pattern.T, weights, moment, activations, residual, upstream, norm_gain.reshape(n_col, 128))
 
 
 def body(activations, residual, upstream, norm_gain, params, momentum, pattern, step_index):

time: 253 us -> 255 us (level)
  Pallas kernels: 245 us -> 251 us
    pallas_call x1, Pallas kernels: 245 us -> 251 us  [two_steps(): pl.pallas_call(partial(steps_kernel, hops, scaling), out_shape=[jax.Shape...]
where the time goes in v3:
time: 255 us; the launch traced here: 256 us
  Pallas kernels  251 us (98%)
  local copies, waits for them, and re-layouts  3.79 us (1%)
    pallas_call x1, Pallas kernels, two_steps(): pl.pallas_call(partial(steps_kernel, hops, scaling), out_shape=[jax.Shape...  251 us

profile of v3, /device:TPU:8, one launch (start us, length us, event | category | flops | bytes accessed | tf_op | source)
XLA Modules:
  0.0 255.7 jit_solution(17494732661167423704)
XLA Ops:
  1.3 1.7 copy_bitcast_fusion.2
  3.0 250.6 %conditional.1 = ((f32[40,5,8,128]{3,2,1,0:T(8,128)S(1)}, f32[40,5,8,128]{3,2,1,0:T(8,128)S(1)})) conditional(s32[]{:T(128)} %clamp.3, (s32[40,5]{0,1:T(8,128)}, f32[5120]{0:T(1024)}, f32[40,5,8,128]{3,2,1,0:T(8,128)S(1)}, f32[40,5,8,128]{3,2,1,0:T(8,128)S(1)}, bf16[1,2,176,2560]{3,2,1,0:T(8,128)(2,1)}, ...), branch_computations={%region_0.1_spmd, %region_1.2_spmd, %region_2.3_spmd} | conditional | bytes 8 | solution.py:385
  3.0 250.5 %two_steps.3 = (f32[40,5,8,128]{3,2,1,0:T(8,128)S(1)}, f32[40,5,8,128]{3,2,1,0:T(8,128)S(1)}) custom-call(s32[5,40]{1,0:T(8,128)} %bitcast.30, f32[40,5,8,128]{3,2,1,0:T(8,128)S(1)} %get-tuple-element.43.w_in, f32[40,5,8,128]{3,2,1,0:T(8,128)S(1)} %get-tuple-element.44.m_in, bf16[1,2,176,2560]{3,2,1,0:T(8,128)(2,1)} %get-tuple-element.45.act_hbm, ...), custom_call_target="tpu_custom_call" | custom-call | tf_op jit(solution)/shard_map/cond/branch_0_fun/two_steps/pallas_call | solution.py:340
  253.6 1.0 copy.19
  254.6 1.0 copy.18
